TPU v7x, 32 devices: a whole 2x2x4 slice. The times are simulated.
32 devices in a mesh: groups: 1, row: 32 (over z, y, x, core), col: 1.
Axes of the slice: x: 2, y: 2, z: 4, core: 2. Of those that a mesh axis runs over, the one named last changes fastest.
Arguments:
- pair_map: bfloat16 [128, 128, 288], P(('groups', 'col'), 'row'), may hold values from -10 to 10
- row_gain: float32 [288], replicated, may hold values from 0.1 to 1.9
- row_proj: bfloat16 [288, 1152], replicated, may hold values from -0.5 to 0.5
- row_gate_bias: float32 [288], replicated, may hold values from -4 to 4
- row_out: bfloat16 [288, 288], replicated, may hold values from -0.375 to 0.375
- col_gain: float32 [288], replicated, may hold values from 0.1 to 1.9
- col_proj: bfloat16 [288, 1152], replicated, may hold values from -0.5 to 0.5
- col_gate_bias: float32 [288], replicated, may hold values from -4 to 4
- col_out: bfloat16 [288, 288], replicated, may hold values from -0.375 to 0.375
Outputs:
- updated_map: bfloat16 [128, 128, 288], P(('groups', 'col'), 'row')
All inputs are finite; a program needn't handle non-finite values.
Results may differ from a plain program's by a relative error of at most 0.006.
Values may be sent and summed in bfloat16 or wider, within the bound.
A program may use at most 64 MiB of HBM per device.

v0:
```python
import jax
import jax.numpy as jnp
from jax import lax
from jax.sharding import PartitionSpec as P

HEADS = 8


def attend(block, gain, w_proj, gate_bias, w_out, keys_first):
    width = block.shape[-1]
    head_count = HEADS
    per_head_width = width // head_count
    source = block.astype(jnp.float32)
    average = jnp.mean(source, -1, keepdims=True)
    centred = source - average
    spread = jnp.mean(centred * centred, -1, keepdims=True)
    normed = (centred * lax.rsqrt(spread + 1e-05) * gain).astype(jnp.bfloat16)
    projected = jnp.dot(normed.reshape(-1, width), w_proj, preferred_element_type=jnp.float32)
    projected = projected.reshape(block.shape[:-1] + (4 * width,))
    query_rows = projected[..., :width].astype(jnp.bfloat16)
    key_rows = projected[..., width : 2 * width].astype(jnp.bfloat16)
    value_rows = projected[..., 2 * width : 3 * width].astype(jnp.bfloat16)
    gating = jax.nn.sigmoid(projected[..., 3 * width :] + gate_bias)
    score_scale_factor = 1.0 / per_head_width**0.5
    head_outputs = []
    for head_index in range(head_count):
        lower_start = head_index * per_head_width
        query_slice = query_rows[..., lower_start : lower_start + per_head_width]
        key_slice = key_rows[..., lower_start : lower_start + per_head_width]
        value_slice = value_rows[..., lower_start : lower_start + per_head_width]
        if keys_first:
            logit_matrix = jnp.einsum(
                "ots,pts->top", query_slice, key_slice, preferred_element_type=jnp.float32
            )
        else:
            logit_matrix = jnp.einsum(
                "duv,dtv->dut", query_slice, key_slice, preferred_element_type=jnp.float32
            )
        softmax_weights = jax.nn.softmax(logit_matrix * score_scale_factor, -1).astype(jnp.bfloat16)
        if keys_first:
            head_outputs.append(
                jnp.einsum(
                    "cho,oct->hct", softmax_weights, value_slice, preferred_element_type=jnp.float32
                )
            )
        else:
            head_outputs.append(
                jnp.einsum(
                    "twn,tnl->twl", softmax_weights, value_slice, preferred_element_type=jnp.float32
                )
            )
    mixed = jnp.concatenate(head_outputs, -1)
    gated = (mixed * gating).astype(jnp.bfloat16)
    changes = jnp.dot(gated.reshape(-1, width), w_out, preferred_element_type=jnp.float32).reshape(
        block.shape
    )
    return (source + changes).astype(jnp.bfloat16)


def per_device(
    pair_map, row_gain, row_proj, row_gate_bias, row_out, col_gain, col_proj, col_gate_bias, col_out
):
    local_rows, local_cols, width = pair_map.shape
    row_devices = lax.axis_size("row")
    tiles = pair_map.reshape(row_devices, local_rows // row_devices, local_cols, width)
    grouped = lax.all_to_all(tiles, "row", split_axis=0, concat_axis=2, tiled=True)
    row_count = grouped.shape[1]
    key_count = grouped.shape[2]
    done = attend(
        grouped.reshape(row_count, key_count, width),
        row_gain,
        row_proj,
        row_gate_bias,
        row_out,
        False,
    )
    rows_done = done.reshape(1, row_count, key_count, width)
    row_count = rows_done.shape[1]
    key_count = rows_done.shape[2]
    returned = lax.all_to_all(rows_done, "row", split_axis=2, concat_axis=0, tiled=True)
    grouped = returned.reshape(row_devices, 1, row_count, local_cols, width)
    columns = lax.all_to_all(grouped, "col", split_axis=3, concat_axis=1, tiled=True)
    flattened = columns.reshape(-1, columns.shape[3], width)
    col_done = attend(flattened, col_gain, col_proj, col_gate_bias, col_out, True).reshape(
        columns.shape
    )
    restored = lax.all_to_all(col_done, "col", split_axis=1, concat_axis=3, tiled=True)
    return restored.reshape(local_rows, local_cols, width)


def solution(mesh):
    return jax.shard_map(
        per_device,
        mesh=mesh,
        in_specs=(P(("groups", "col"), "row", None), P(), P(), P(), P(), P(), P(), P(), P()),
        out_specs=P(("groups", "col"), "row", None),
        check_vma=False,
    )
```

profile of v0, /device:TPU:0, one launch (start us, length us, event | category | flops | bytes accessed | tf_op | source)
XLA Modules:
  0.0 101.8 jit_solution(13849073327140385981)
XLA Ops:
  0.0 1.3 %copy.200 = bf16[128,4,288]{2,1,0:T(4,128)(2,1)S(1)} copy(bf16[128,4,288]{0,2,1:T(8,128)(2,1)} %param.9) | data formatting | bytes 589824 | tf_op args[0]
  1.3 20.4 %all_to_all.8 = bf16[32,4,4,288]{3,2,1,0:T(4,128)(2,1)S(1)} all-to-all(bf16[32,4,4,288]{3,2,1,0:T(4,128)(2,1)S(1)} %bitcast.83), channel_id=1, replica_groups=mesh['groups'=1,'row'=32,'col'=1] {'row'}, dimensions={0} | all-to-all | bytes 589824 | tf_op jit(solution)/shard_map/all_to_all | solution.py:66
  24.1 2.2 %fusion.249 = (bf16[4,128,1152]{2,1,0:T(8,128)(2,1)S(1)}, f32[4,128,1152]{2,1,0:T(8,128)}) fusion(bf16[288,1152]{1,0:T(8,128)(2,1)S(1)} %copy-done, bf16[4,128,288]{2,0,1:T(4,128)(2,1)S(1)} %multiply_convert_fusion.1), kind=kOutput, calls=%fused_computation.237 | convolution fusion | flops 340328448 | bytes 4497408 | tf_op jit(solution)/shard_map/dot_general | solution.py:18
  29.0 1.0 convolution_multiply_fusion.11
  30.0 1.0 convolution_multiply_fusion.12
  32.0 1.0 convolution_multiply_fusion.13
  36.5 1.3 %fusion.83 = f32[4,128,36]{2,1,0:T(8,128)S(1)} fusion(bf16[4,128,1152]{2,1,0:T(8,128)(2,1)S(1)} %get-tuple-element.5, f32[4,128]{1,0:T(4,128)S(1)} %fusion.270, f32[4,128,128]{1,2,0:T(8,128)} %convolution_multiply_fusion.11), kind=kOutput, calls=%fused_computation.131 | convolution fusion | flops 4915839 | bytes 731136 | tf_op jit(solution)/shard_map/twn,tnl->twl/dot_general | solution.py:48
  37.9 1.3 %fusion.82 = f32[4,128,36]{2,1,0:T(8,128)S(1)} fusion(bf16[4,128,1152]{2,1,0:T(8,128)(2,1)S(1)} %get-tuple-element.5, f32[4,128]{1,0:T(4,128)S(1)} %fusion.265, f32[4,128,128]{1,2,0:T(8,128)} %convolution_multiply_fusion.12), kind=kOutput, calls=%fused_computation.130 | convolution fusion | flops 4915839 | bytes 731136 | tf_op jit(solution)/shard_map/twn,tnl->twl/dot_general | solution.py:48
  39.2 1.3 %fusion.85 = f32[4,128,36]{2,1,0:T(8,128)S(1)} fusion(bf16[4,128,1152]{2,1,0:T(8,128)(2,1)S(1)} %get-tuple-element.5, f32[4,128]{1,0:T(4,128)S(1)} %fusion.280, f32[4,128,128]{1,2,0:T(8,128)} %convolution_multiply_fusion.9), kind=kOutput, calls=%fused_computation.133 | convolution fusion | flops 4915839 | bytes 731136 | tf_op jit(solution)/shard_map/twn,tnl->twl/dot_general | solution.py:48
  40.5 2.0 %fusion.81 = f32[4,128,36]{2,1,0:T(8,128)} fusion(bf16[4,128,1152]{2,1,0:T(8,128)(2,1)S(1)} %get-tuple-element.5, f32[4,128]{1,0:T(4,128)S(1)} %fusion.260, f32[4,128,128]{1,2,0:T(8,128)} %convolution_multiply_fusion.13), kind=kOutput, calls=%fused_computation.129 | convolution fusion | flops 4915839 | bytes 731136 | tf_op jit(solution)/shard_map/twn,tnl->twl/dot_general | solution.py:48
  42.5 2.0 %fusion.86 = f32[4,128,36]{2,1,0:T(8,128)} fusion(bf16[4,128,1152]{2,1,0:T(8,128)(2,1)S(1)} %get-tuple-element.5, f32[4,128]{1,0:T(4,128)S(1)} %fusion.285, f32[4,128,128]{1,2,0:T(8,128)} %convolution_multiply_fusion.8), kind=kOutput, calls=%fused_computation.134 | convolution fusion | flops 4915839 | bytes 731136 | tf_op jit(solution)/shard_map/twn,tnl->twl/dot_general | solution.py:48
  44.6 2.0 %fusion.80 = f32[4,128,36]{2,1,0:T(8,128)} fusion(bf16[4,128,1152]{2,1,0:T(8,128)(2,1)S(1)} %get-tuple-element.5, f32[4,128]{1,0:T(4,128)S(1)} %fusion.255, f32[4,128,128]{1,2,0:T(8,128)} %convolution_multiply_fusion.14), kind=kOutput, calls=%fused_computation.128 | convolution fusion | flops 4915839 | bytes 731136 | tf_op jit(solution)/shard_map/twn,tnl->twl/dot_general | solution.py:48
  46.6 2.1 %fusion.79 = f32[4,128,36]{2,1,0:T(8,128)} fusion(bf16[4,128,1152]{2,1,0:T(8,128)(2,1)S(1)} %get-tuple-element.5, f32[4,128]{1,0:T(4,128)S(1)} %fusion.250, f32[4,128,128]{1,2,0:T(8,128)} %convolution_multiply_fusion.15), kind=kOutput, calls=%fused_computation.127 | convolution fusion | flops 4915839 | bytes 731136 | tf_op jit(solution)/shard_map/twn,tnl->twl/dot_general | solution.py:48
  48.7 1.0 fusion.84
  49.7 1.9 %concatenate.6 = f32[4,128,288]{2,1,0:T(8,128)S(1)} concatenate(f32[4,128,36]{2,1,0:T(8,128)} %fusion.79, f32[4,128,36]{2,1,0:T(8,128)} %fusion.80, f32[4,128,36]{2,1,0:T(8,128)} %fusion.81, f32[4,128,36]{2,1,0:T(8,128)S(1)} %fusion.82, f32[4,128,36]{2,1,0:T(8,128)S(1)} %fusion.83, f32[4,128,36]{2,1,0:T(8,128)} %fusion.84, f32[4,128,36]{2,1,0:T(8,128)S(1)} %fusion.85, ...), dimensions={2} | concatenate | bytes 1179648 | tf_op jit(solution)/shard_map/concatenate | solution.py:52
  51.6 1.7 %fusion.34 = bf16[1,4,128,288]{2,3,1,0:T(8,128)(2,1)S(1)} fusion(f32[4,128,288]{1,2,0:T(8,128)S(1)} %copy.252, f32[4,128,288]{2,1,0:T(8,128)S(1)} %concatenate.6, f32[4,128,1152]{2,1,0:T(8,128)} %get-tuple-element.6, f32[288]{0:T(512)S(1)} %copy-done.6, bf16[288,288]{1,0:T(8,128)(2,1)S(1)} %copy-done.4), kind=kOutput, calls=%fused_computation.36 | convolution fusion | flops 86114304 | bytes 2428032 | tf_op jit(solution)/shard_map/dot_general | solution.py:54
  53.6 15.6 %all_to_all.9 = bf16[1,4,128,288]{3,1,0,2:T(4,128)(2,1)S(1)} all-to-all(bf16[1,4,128,288]{3,1,0,2:T(4,128)(2,1)S(1)} %copy.253), channel_id=1, replica_groups=mesh['groups'=1,'row'=32,'col'=1] {'row'}, dimensions={2} | all-to-all | bytes 589824 | tf_op jit(solution)/shard_map/all_to_all | solution.py:80
  71.9 2.2 %fusion.290 = (bf16[128,4,1152]{2,0,1:T(8,128)(2,1)S(1)}, f32[128,4,1152]{2,0,1:T(8,128)}) fusion(bf16[288,1152]{1,0:T(8,128)(2,1)S(1)} %copy-done.1, bf16[128,4,288]{2,1,0:T(4,128)(2,1)S(1)} %multiply_convert_fusion), kind=kOutput, calls=%fused_computation.246 | convolution fusion | flops 340328448 | bytes 4497408 | tf_op jit(solution)/shard_map/dot_general | solution.py:18
  76.7 1.0 convolution_multiply_fusion.3
  78.7 1.0 convolution_multiply_fusion.4
  79.7 1.0 convolution_multiply_fusion
  81.7 1.0 convolution_multiply_fusion.6
  84.2 1.3 %convolution_bitcast_fusion.3 = f32[128,4,36]{2,0,1:T(8,128)S(1)} fusion(bf16[128,4,1152]{2,0,1:T(8,128)(2,1)S(1)} %get-tuple-element.7, f32[4,128]{1,0:T(4,128)S(1)} %fusion.311, f32[4,128,128]{1,2,0:T(8,128)} %convolution_multiply_fusion.3), kind=kOutput, calls=%fused_computation.72 | convolution fusion | flops 4915839 | bytes 731136 | tf_op jit(solution)/shard_map/cho,oct->hct/dot_general | solution.py:42
  85.6 1.3 %convolution_bitcast_fusion.1 = f32[128,4,36]{2,0,1:T(8,128)S(1)} fusion(bf16[128,4,1152]{2,0,1:T(8,128)(2,1)S(1)} %get-tuple-element.7, f32[4,128]{1,0:T(4,128)S(1)} %fusion.321, f32[4,128,128]{1,2,0:T(8,128)} %convolution_multiply_fusion.1), kind=kOutput, calls=%fused_computation.70 | convolution fusion | flops 4915839 | bytes 731136 | tf_op jit(solution)/shard_map/cho,oct->hct/dot_general | solution.py:42
  86.9 1.3 %convolution_bitcast_fusion.4 = f32[128,4,36]{2,0,1:T(8,128)S(1)} fusion(bf16[128,4,1152]{2,0,1:T(8,128)(2,1)S(1)} %get-tuple-element.7, f32[4,128]{1,0:T(4,128)S(1)} %fusion.306, f32[4,128,128]{1,2,0:T(8,128)} %convolution_multiply_fusion.4), kind=kOutput, calls=%fused_computation.73 | convolution fusion | flops 4915839 | bytes 731136 | tf_op jit(solution)/shard_map/cho,oct->hct/dot_general | solution.py:42
  88.2 2.0 %convolution_bitcast_fusion = f32[128,4,36]{2,0,1:T(8,128)} fusion(bf16[128,4,1152]{2,0,1:T(8,128)(2,1)S(1)} %get-tuple-element.7, f32[4,128]{1,0:T(4,128)S(1)} %fusion.326, f32[4,128,128]{1,2,0:T(8,128)} %convolution_multiply_fusion), kind=kOutput, calls=%fused_computation.69 | convolution fusion | flops 4915839 | bytes 731136 | tf_op jit(solution)/shard_map/cho,oct->hct/dot_general | solution.py:42
  90.2 2.0 %convolution_bitcast_fusion.5 = f32[128,4,36]{2,0,1:T(8,128)} fusion(bf16[128,4,1152]{2,0,1:T(8,128)(2,1)S(1)} %get-tuple-element.7, f32[4,128]{1,0:T(4,128)S(1)} %fusion.301, f32[4,128,128]{1,2,0:T(8,128)} %convolution_multiply_fusion.5), kind=kOutput, calls=%fused_computation.74 | convolution fusion | flops 4915839 | bytes 731136 | tf_op jit(solution)/shard_map/cho,oct->hct/dot_general | solution.py:42
  92.3 2.1 %convolution_bitcast_fusion.6 = f32[128,4,36]{2,0,1:T(8,128)} fusion(bf16[128,4,1152]{2,0,1:T(8,128)(2,1)S(1)} %get-tuple-element.7, f32[4,128]{1,0:T(4,128)S(1)} %fusion.296, f32[4,128,128]{1,2,0:T(8,128)} %convolution_multiply_fusion.6), kind=kOutput, calls=%fused_computation.75 | convolution fusion | flops 4915839 | bytes 731136 | tf_op jit(solution)/shard_map/cho,oct->hct/dot_general | solution.py:42
  94.4 2.0 %convolution_bitcast_fusion.2 = f32[128,4,36]{2,0,1:T(8,128)} fusion(bf16[128,4,1152]{2,0,1:T(8,128)(2,1)S(1)} %get-tuple-element.7, f32[4,128]{1,0:T(4,128)S(1)} %fusion.316, f32[4,128,128]{1,2,0:T(8,128)} %convolution_multiply_fusion.2), kind=kOutput, calls=%fused_computation.71 | convolution fusion | flops 4915839 | bytes 731136 | tf_op jit(solution)/shard_map/cho,oct->hct/dot_general | solution.py:42
  96.4 1.0 convolution_bitcast_fusion.7
  97.4 1.9 %concatenate.7 = f32[128,4,288]{2,0,1:T(8,128)S(1)} concatenate(f32[128,4,36]{2,0,1:T(8,128)} %convolution_bitcast_fusion.7, f32[128,4,36]{2,0,1:T(8,128)} %convolution_bitcast_fusion.6, f32[128,4,36]{2,0,1:T(8,128)} %convolution_bitcast_fusion.5, f32[128,4,36]{2,0,1:T(8,128)S(1)} %convolution_bitcast_fusion.4, f32[128,4,36]{2,0,1:T(8,128)S(1)} %convolution_bitcast_fusion.3, ...), dimensions={2} | concatenate | bytes 1179648 | tf_op jit(solution)/shard_map/concatenate | solution.py:52
  99.4 2.4 %fusion.17 = bf16[128,4,288]{0,2,1:T(8,128)(2,1)} fusion(f32[128,4,288]{0,2,1:T(8,128)S(1)} %copy.305, f32[128,4,288]{2,0,1:T(8,128)S(1)} %concatenate.7, f32[128,4,1152]{2,0,1:T(8,128)} %get-tuple-element.8, f32[288]{0:T(512)S(1)} %copy-done.7, bf16[288,288]{1,0:T(8,128)(2,1)S(1)} %copy-done.5), kind=kOutput, calls=%fused_computation.19 | convolution fusion | flops 86114304 | bytes 2428032 | tf_op jit(solution)/shard_map/dot_general | solution.py:54
  (68 shorter events, 18.6 us)
Async XLA Ops:
  0.0 24.1 %copy-start = (bf16[288,1152]{1,0:T(8,128)(2,1)S(1)}, bf16[288,1152]{1,0:T(8,128)(2,1)}, u32[]{:S(2)}) copy-start(bf16[288,1152]{1,0:T(8,128)(2,1)} %param.11) | copy-start | bytes 1990660
  23.1 0.7 copy-start.2
  49.7 2.0 %copy-start.4 = (bf16[288,288]{1,0:T(8,128)(2,1)S(1)}, bf16[288,288]{1,0:T(8,128)(2,1)}, u32[]{:S(2)}) copy-start(bf16[288,288]{1,0:T(8,128)(2,1)} %param.13) | copy-start | bytes 497668
  49.7 2.0 %copy-start.6 = (f32[288]{0:T(512)S(1)}, f32[288]{0:T(512)}, u32[]{:S(2)}) copy-start(f32[288]{0:T(512)} %param.12) | copy-start | bytes 3460
  70.0 1.0 %copy-start.3 = (f32[288]{0:T(512)S(1)}, f32[288]{0:T(512)}, u32[]{:S(2)}) copy-start(f32[288]{0:T(512)} %param.14) | copy-start | bytes 3460
  70.8 1.1 %copy-start.1 = (bf16[288,1152]{1,0:T(8,128)(2,1)S(1)}, bf16[288,1152]{1,0:T(8,128)(2,1)}, u32[]{:S(2)}) copy-start(bf16[288,1152]{1,0:T(8,128)(2,1)} %param.15) | copy-start | bytes 1990660
  97.4 2.0 %copy-start.5 = (bf16[288,288]{1,0:T(8,128)(2,1)S(1)}, bf16[288,288]{1,0:T(8,128)(2,1)}, u32[]{:S(2)}) copy-start(bf16[288,288]{1,0:T(8,128)(2,1)} %param.17) | copy-start | bytes 497668
  97.4 2.0 %copy-start.7 = (f32[288]{0:T(512)S(1)}, f32[288]{0:T(512)}, u32[]{:S(2)}) copy-start(f32[288]{0:T(512)} %param.16) | copy-start | bytes 3460
where the time goes:
time: 102 us
  matrix products  54.5 us (53%)
  blocking collectives  36 us (35%)
  local copies, waits for them, and re-layouts  8.35 us (8%)
  other arithmetic  2.63 us (3%)
    all_to_all x1, blocking collectives, per_device(): lax.all_to_all(tiles, 'row', split_axis=0, concat_axis=2, tiled=True)  20.4 us
    all_to_all x1, blocking collectives, per_device(): lax.all_to_all(rows_done, 'row', split_axis=2, concat_axis=0, tiled=True)  15.6 us
    dot_general x8, matrix products, attend(): jnp.einsum('cho,oct->hct', softmax_weights, value_slice, preferred_elemen...  13.1 us
    dot_general x8, matrix products, attend(): jnp.einsum('twn,tnl->twl', softmax_weights, value_slice, preferred_elemen...  13.1 us
    dot_general x8, matrix products, attend(): jnp.einsum('ots,pts->top', query_slice, key_slice, preferred_element_type...  7.18 us
    dot_general x8, matrix products, attend(): jnp.einsum('duv,dtv->dut', query_slice, key_slice, preferred_element_type...  7.18 us
    sub x16, matrix products, attend(): jax.nn.softmax(logit_matrix * score_scale_factor, -1).astype(jnp.bfloat16)  5.34 us
    dot_general x2, matrix products, attend(): jnp.dot(normed.reshape(-1, width), w_proj, preferred_element_type=jnp.flo...  4.41 us

commit v1 on v0

v1 whole, which is shorter than its diff:
```python
import functools
import math

import jax
import jax.numpy as jnp
from jax import lax
from jax.experimental import pallas as pl
from jax.experimental.pallas import tpu as pltpu
from jax.sharding import PartitionSpec as P

HEADS = 8
LANES = 128
F32 = jnp.float32
BF16 = jnp.bfloat16
MESH = pl.DeviceIdType.MESH


def ceil_to(value, step):
    return -(-value // step) * step


def nt(a, b):
    return lax.dot_general(a, b, (((1,), (1,)), ((), ())), preferred_element_type=F32)


def tn(a, b):
    return lax.dot_general(a, b, (((0,), (0,)), ((), ())), preferred_element_type=F32)


def nn(a, b):
    return jnp.dot(a, b, preferred_element_type=F32)


class Sizes:
    def __init__(self, width):
        self.width = width
        self.head = width // HEADS
        self.pad_head = ceil_to(self.head + 1, 16)
        self.rows = HEADS * self.pad_head
        self.lanes = ceil_to(width, LANES)
        self.chunks = self.lanes // LANES

    def weight_scratch(self):
        return [
            pltpu.VMEM((self.width, HEADS * LANES), BF16),
            pltpu.VMEM((self.width, HEADS * LANES), BF16),
            pltpu.VMEM((self.rows, self.width), BF16),
            pltpu.VMEM((self.rows, self.width), BF16),
            pltpu.VMEM((self.rows, self.lanes), BF16),
            pltpu.VMEM((self.rows, 1), F32),
        ]

    def token_scratch(self, tokens):
        return [pltpu.VMEM((self.chunks, tokens, LANES), F32)] * 2


def prepare(sz, weights, packed):
    proj, bias, out = weights
    wq, wk, wvt, wgt, wo, bias_col = packed

    def window(block):
        start = block * sz.width
        low = start // LANES * LANES
        high = min(ceil_to(start + sz.width, LANES), 4 * sz.width)
        return proj[:, low:high], start - low, high - low

    for block, ref in ((0, wq), (1, wk)):
        part, shift, size = window(block)
        source = lax.broadcasted_iota(jnp.int32, (size, HEADS * LANES), 0) - shift
        lane = lax.broadcasted_iota(jnp.int32, (size, HEADS * LANES), 1)
        inner = lane % LANES
        hit = (inner < sz.head) & (source == lane // LANES * sz.head + inner)
        ref[...] = nn(part, jnp.where(hit, 1.0, 0.0).astype(BF16)).astype(BF16)

    def row_hits(size, shift):
        source = lax.broadcasted_iota(jnp.int32, (sz.rows, size), 1) - shift
        row = lax.broadcasted_iota(jnp.int32, (sz.rows, size), 0)
        inner = row % sz.pad_head
        return (inner < sz.head) & (source == row // sz.pad_head * sz.head + inner)

    for block, ref in ((2, wvt), (3, wgt)):
        part, shift, size = window(block)
        pick = jnp.where(row_hits(size, shift), 1.0, 0.0).astype(BF16)
        ref[...] = nt(pick, part).astype(BF16)
    hits = row_hits(sz.width, 0)
    pick = jnp.where(hits, 1.0, 0.0).astype(BF16)
    wo[...] = jnp.zeros_like(wo)
    wo[:, : sz.width] = nn(pick, out[...]).astype(BF16)
    bias_col[...] = jnp.sum(jnp.where(hits, bias[...], 0.0), axis=1, keepdims=True)


def attend(sz, groups, length, start_of, stride, per_group, gain, packed, xs, ys):
    wq, wk, wvt, wgt, wo, bias_col = packed
    run = length // per_group
    factor = math.log2(math.e) / sz.head**0.5
    lane = lax.broadcasted_iota(jnp.int32, (1, sz.lanes), 1)
    inside = lane < sz.width
    feature = lax.broadcasted_iota(jnp.int32, (sz.rows, 1), 0)
    ones_row = jnp.where(feature % sz.pad_head == sz.head, 1.0, 0.0)
    for group in range(groups):
        places = [pl.ds(start_of(group, c), run, stride=stride) for c in range(per_group)]
        x = jnp.concatenate(
            [
                jnp.concatenate([xs[k, place, :] for place in places], axis=0)
                for k in range(sz.chunks)
            ],
            axis=1,
        )
        mean = jnp.sum(x, axis=1, keepdims=True) * (1.0 / sz.width)
        centred = jnp.where(inside, x - mean, 0.0)
        spread = jnp.sum(centred * centred, axis=1, keepdims=True) * (1.0 / sz.width)
        normed = centred[:, : sz.width] * lax.rsqrt(spread + 1e-05) * gain[...]
        normed = normed.astype(BF16)
        q = (nn(normed, wq[...]) * factor).astype(BF16)
        k = nn(normed, wk[...]).astype(BF16)
        vt = (nt(wvt[...], normed) + ones_row).astype(BF16)
        gate = jax.nn.sigmoid(nt(wgt[...], normed) + bias_col[...])
        pieces = []
        for head in range(HEADS):
            lanes = slice(head * LANES, (head + 1) * LANES)
            rows = slice(head * sz.pad_head, (head + 1) * sz.pad_head)
            scores = nt(k[:, lanes], q[:, lanes])
            top = jnp.max(scores, axis=0, keepdims=True)
            weight = jnp.exp2(scores - top).astype(BF16)
            mixed = nn(vt[rows], weight)
            total = mixed[sz.head : sz.head + 1]
            pieces.append((mixed * (1.0 / total) * gate[rows]).astype(BF16))
        gated = jnp.concatenate(pieces, axis=0)
        y = x + tn(gated, wo[...])
        for k_chunk in range(sz.chunks):
            part = y[:, k_chunk * LANES : (k_chunk + 1) * LANES]
            for c, place in enumerate(places):
                ys[k_chunk, place, :] = part[c * run : (c + 1) * run]


def spread_tokens(sz, source, xs):
    tokens = xs.shape[1]
    flat = source[...].astype(F32).reshape(tokens, sz.width)
    for k in range(sz.chunks):
        part = flat[:, k * LANES : min((k + 1) * LANES, sz.width)]
        if part.shape[1] < LANES:
            pad = jnp.zeros((tokens, LANES - part.shape[1]), F32)
            part = jnp.concatenate([part, pad], axis=1)
        xs[k] = part


def gather_tokens(sz, ys, target):
    shape = target.shape
    for k in range(sz.chunks):
        low, high = k * LANES, min((k + 1) * LANES, sz.width)
        part = ys[k][:, : high - low]
        target[..., low:high] = part.reshape(shape[:-1] + (high - low,)).astype(BF16)


def row_kernel(
    sz, n, rows, cols, x_ref, gain, proj, bias, out_w, result, got, back, xs, ys, *rest
):
    packed = rest[:6]
    send_a, recv_a, send_b, recv_b, local_sem = rest[6:]
    me = lax.axis_index("row")

    barrier = pltpu.get_barrier_semaphore()

    def greet(step, carry):
        peer = lax.rem(me + step, n)
        pl.semaphore_signal(barrier, inc=1, device_id={"row": peer}, device_id_type=MESH)
        return carry

    lax.fori_loop(1, n, greet, 0)
    pl.semaphore_wait(barrier, n - 1)

    def copy(source, target, send, recv, peer, slot):
        return pltpu.make_async_remote_copy(
            src_ref=source.at[peer],
            dst_ref=target.at[slot],
            send_sem=send.at[peer],
            recv_sem=recv.at[slot],
            device_id={"row": peer},
            device_id_type=MESH,
        )

    def exchange(source, target, send, recv, work):
        def start(step, carry):
            peer = lax.rem(me + step, n)
            copy(source, target, send, recv, peer, me).start()
            return carry

        lax.fori_loop(1, n, start, 0)
        own = pltpu.make_async_copy(source.at[me], target.at[me], local_sem)
        own.start()
        work()
        own.wait()

        def finish(step, carry):
            peer = lax.rem(me + step, n)
            copy(source, target, send, recv, peer, me).wait_send()
            copy(source, target, send, recv, peer, peer).wait_recv()
            return carry

        lax.fori_loop(1, n, finish, 0)

    exchange(x_ref, got, send_a, recv_a, lambda: prepare(sz, (proj, bias, out_w), packed))
    spread_tokens(sz, got, xs)
    block = rows * cols
    attend(
        sz, rows, n * cols, lambda g, c: g * cols + c, block, cols, gain, packed, xs, ys
    )
    gather_tokens(sz, ys, back)
    exchange(back, result, send_b, recv_b, lambda: None)


def col_kernel(sz, cols, x_ref, gain, proj, bias, out_w, result, xs, ys, *packed):
    prepare(sz, (proj, bias, out_w), packed)
    spread_tokens(sz, x_ref, xs)
    length = xs.shape[1] // cols
    attend(sz, cols, length, lambda g, c: g, cols, 1, gain, packed, xs, ys)
    gather_tokens(sz, ys, result)


VMEM = pl.BlockSpec(memory_space=pltpu.VMEM)


def per_device(
    pair_map, row_gain, row_proj, row_gate_bias, row_out, col_gain, col_proj, col_gate_bias, col_out
):
    local_rows, local_cols, width = pair_map.shape
    n = lax.axis_size("row")
    sz = Sizes(width)
    rows = local_rows // n
    tokens = local_rows * local_cols
    block = rows * local_cols
    shape = (n, block, width)
    done = pl.pallas_call(
        functools.partial(row_kernel, sz, n, rows, local_cols),
        out_shape=jax.ShapeDtypeStruct(shape, BF16),
        in_specs=[VMEM] * 5,
        out_specs=VMEM,
        scratch_shapes=[pltpu.VMEM(shape, BF16)] * 2
        + sz.token_scratch(tokens)
        + sz.weight_scratch()
        + [pltpu.SemaphoreType.DMA((n,))] * 4
        + [pltpu.SemaphoreType.DMA],
        compiler_params=pltpu.CompilerParams(collective_id=0, has_side_effects=True),
        name="row_attention",
    )(
        pair_map.reshape(shape),
        row_gain.reshape(1, width),
        row_proj,
        row_gate_bias.reshape(1, width),
        row_out,
    )
    splits = lax.axis_size("col")
    if splits > 1:
        done = done.reshape(local_rows, local_cols, width)
        done = lax.all_to_all(done, "col", split_axis=1, concat_axis=0, tiled=True)
    cols = local_cols // splits
    full = tokens // cols
    updated = pl.pallas_call(
        functools.partial(col_kernel, sz, cols),
        out_shape=jax.ShapeDtypeStruct(shape, BF16),
        in_specs=[VMEM] * 5,
        out_specs=VMEM,
        scratch_shapes=sz.token_scratch(tokens) + sz.weight_scratch(),
        name="col_attention",
    )(
        done.reshape(shape),
        col_gain.reshape(1, width),
        col_proj,
        col_gate_bias.reshape(1, width),
        col_out,
    )
    if splits > 1:
        updated = updated.reshape(full, cols, width)
        updated = lax.all_to_all(updated, "col", split_axis=0, concat_axis=1, tiled=True)
    return updated.reshape(local_rows, local_cols, width)


def solution(mesh):
    return jax.shard_map(
        per_device,
        mesh=mesh,
        in_specs=(P(("groups", "col"), "row", None), P(), P(), P(), P(), P(), P(), P(), P()),
        out_specs=P(("groups", "col"), "row", None),
        check_vma=False,
    )
```

time: 102 us -> 55.7 us (0.55)
  the two profiles are of different devices: /device:TPU:0 before, /device:TPU:29 now
where the time goes in v1:
time: 55.7 us; the launch traced here: 55.4 us
  Pallas kernels  48.6 us (87%)
  local copies, waits for them, and re-layouts  6.75 us (12%)
    pallas_call x1, Pallas kernels, per_device(): pl.pallas_call(functools.partial(row_kernel, sz, n, rows, local_cols), ou...  37.1 us
    pallas_call x1, Pallas kernels, per_device(): pl.pallas_call(functools.partial(col_kernel, sz, cols), out_shape=jax.Sha...  11.5 us
    reshape x2, local copies, waits for them, and re-layouts, per_device(): return updated.reshape(local_rows, local_cols, width)  2.09 us
    unnamed x9, local copies, waits for them, and re-layouts  1.44 us

profile of v1, /device:TPU:29, one launch (start us, length us, event | category | flops | bytes accessed | tf_op | source)
XLA Modules:
  0.0 55.4 jit_solution(11671598242299043434)
XLA Ops:
  0.0 1.2 %copy.12 = bf16[128,4,288]{2,1,0:T(4,128)(2,1)S(1)} copy(bf16[128,4,288]{0,2,1:T(8,128)(2,1)} %param.9) | data formatting | bytes 589824 | tf_op args[0]
  1.2 0.0 copy-start
  1.2 0.9 %reshape.18.x_ref = bf16[32,16,288]{2,1,0:T(8,128)(2,1)} reshape(bf16[128,4,288]{2,1,0:T(4,128)(2,1)S(1)} %copy.12) | data formatting | bytes 589824 | tf_op jit(solution)/shard_map/reshape | solution.py:246
  2.2 0.0 copy-done
  2.2 0.0 copy-start.1
  2.2 0.6 %reshape.19.gain = f32[1,288]{1,0:T(1,128)} reshape(f32[288]{0:T(512)S(1)} %copy-done) | data formatting | bytes 2304 | tf_op jit(solution)/shard_map/reshape | solution.py:247
  2.7 0.1 copy-done.1
  2.8 0.6 %reshape.20.bias = f32[1,288]{1,0:T(1,128)} reshape(f32[288]{0:T(512)S(1)} %copy-done.1) | data formatting | bytes 2304 | tf_op jit(solution)/shard_map/reshape | solution.py:249
  3.4 0.0 copy-start.2
  3.4 37.1 %row_attention.1.x_ref = bf16[32,16,288]{2,1,0:T(8,128)(2,1)} custom-call(bf16[32,16,288]{2,1,0:T(8,128)(2,1)} %reshape.18.x_ref, f32[1,288]{1,0:T(1,128)} %reshape.19.gain, bf16[288,1152]{1,0:T(8,128)(2,1)} %proj.2, f32[1,288]{1,0:T(1,128)} %reshape.20.bias, bf16[288,288]{1,0:T(8,128)(2,1)} %out_w.2), custom_call_target="tpu_custom_call" | custom-call | tf_op jit(solution)/shard_map/row_attention/pallas_call | solution.py:233
  40.5 0.0 copy-done.2
  40.5 0.0 copy-start.3
  40.5 0.6 %reshape.21.gain = f32[1,288]{1,0:T(1,128)} reshape(f32[288]{0:T(512)S(1)} %copy-done.2) | data formatting | bytes 2304 | tf_op jit(solution)/shard_map/reshape | solution.py:267
  41.1 0.1 copy-done.3
  41.2 0.6 %reshape.22.bias = f32[1,288]{1,0:T(1,128)} reshape(f32[288]{0:T(512)S(1)} %copy-done.3) | data formatting | bytes 2304 | tf_op jit(solution)/shard_map/reshape | solution.py:269
  41.8 11.5 %col_attention.1 = bf16[32,16,288]{2,1,0:T(8,128)(2,1)} custom-call(bf16[32,16,288]{2,1,0:T(8,128)(2,1)} %row_attention.1.x_ref, f32[1,288]{1,0:T(1,128)} %reshape.21.gain, bf16[288,1152]{1,0:T(8,128)(2,1)} %proj.3, f32[1,288]{1,0:T(1,128)} %reshape.22.bias, bf16[288,288]{1,0:T(8,128)(2,1)} %out_w.3), custom_call_target="tpu_custom_call" | custom-call | tf_op jit(solution)/shard_map/col_attention/pallas_call | solution.py:258
  53.3 1.1 %reshape.23 = bf16[128,4,288]{2,1,0:T(4,128)(2,1)S(1)} reshape(bf16[32,16,288]{2,1,0:T(8,128)(2,1)} %col_attention.1) | data formatting | bytes 589824 | tf_op jit(solution)/shard_map/reshape | solution.py:275
  54.4 1.0 %copy.13 = bf16[128,4,288]{0,2,1:T(8,128)(2,1)} copy(bf16[128,4,288]{2,1,0:T(4,128)(2,1)S(1)} %reshape.23) | data formatting | bytes 589824 | tf_op jit(solution)/shard_map/reshape | solution.py:275
Async XLA Ops:
  1.2 1.0 %copy-start = (f32[288]{0:T(512)S(1)}, f32[288]{0:T(512)}, u32[]{:S(2)}) copy-start(f32[288]{0:T(512)} %param.10) | copy-start | bytes 3460
  2.2 0.7 %copy-start.1 = (f32[288]{0:T(512)S(1)}, f32[288]{0:T(512)}, u32[]{:S(2)}) copy-start(f32[288]{0:T(512)} %param.12) | copy-start | bytes 3460
  3.4 37.1 %copy-start.2 = (f32[288]{0:T(512)S(1)}, f32[288]{0:T(512)}, u32[]{:S(2)}) copy-start(f32[288]{0:T(512)} %param.14) | copy-start | bytes 3460
  40.5 0.7 %copy-start.3 = (f32[288]{0:T(512)S(1)}, f32[288]{0:T(512)}, u32[]{:S(2)}) copy-start(f32[288]{0:T(512)} %param.16) | copy-start | bytes 3460

commit v2 on v1

v2 whole, which is shorter than its diff:
```python
import functools
import math

import jax
import jax.numpy as jnp
from jax import lax
from jax.experimental import pallas as pl
from jax.experimental.pallas import tpu as pltpu
from jax.sharding import PartitionSpec as P

HEADS = 8
LANES = 128
F32 = jnp.float32
BF16 = jnp.bfloat16
MESH = pl.DeviceIdType.MESH


def ceil_to(value, step):
    return -(-value // step) * step


def nt(a, b):
    return lax.dot_general(a, b, (((1,), (1,)), ((), ())), preferred_element_type=F32)


def tn(a, b):
    return lax.dot_general(a, b, (((0,), (0,)), ((), ())), preferred_element_type=F32)


def nn(a, b):
    return jnp.dot(a, b, preferred_element_type=F32)


class Sizes:
    def __init__(self, width):
        self.width = width
        self.head = width // HEADS
        self.pad_head = ceil_to(self.head + 1, 16)
        self.pad_key = LANES // (LANES // self.head)
        while LANES % self.pad_key:
            self.pad_key += 1
        self.rows = HEADS * self.pad_head
        self.keys = HEADS * self.pad_key
        self.lanes = ceil_to(width, LANES)
        self.chunks = self.lanes // LANES

    def packed_shapes(self):
        return [
            ((self.keys, self.width), BF16),
            ((self.width, self.keys), BF16),
            ((self.rows, self.width), BF16),
            ((self.rows, self.width), BF16),
            ((self.rows, self.lanes), BF16),
            ((self.rows, 1), F32),
        ]

    def work_scratch(self, tokens, length):
        return [
            pltpu.VMEM((self.chunks, tokens, LANES), F32),
            pltpu.VMEM((self.chunks, tokens, LANES), F32),
            pltpu.VMEM((tokens, self.width), BF16),
            pltpu.VMEM((self.keys, tokens), BF16),
            pltpu.VMEM((tokens, self.keys), BF16),
            pltpu.VMEM((self.rows, tokens), BF16),
            pltpu.VMEM((self.rows, tokens), F32),
            pltpu.VMEM((2, length, HEADS * length), F32),
            pltpu.VMEM((2, length, HEADS * length), BF16),
            pltpu.VMEM((self.rows, tokens), BF16),
        ]


def prepare(sz, weights, packed):
    proj, bias, out = weights
    wqt, wk, wvt, wgt, wo, bias_col = packed

    def window(block):
        start = block * sz.width
        low = start // LANES * LANES
        high = min(ceil_to(start + sz.width, LANES), 4 * sz.width)
        return proj[:, low:high], start - low, high - low

    def hits(shape, axis, pad, shift):
        place = lax.broadcasted_iota(jnp.int32, shape, axis)
        source = lax.broadcasted_iota(jnp.int32, shape, 1 - axis) - shift
        inner = place % pad
        return (inner < sz.head) & (source == place // pad * sz.head + inner)

    def pick(*spec):
        return jnp.where(hits(*spec), 1.0, 0.0).astype(BF16)

    part, shift, size = window(1)
    wk[...] = nn(part, pick((size, sz.keys), 1, sz.pad_key, shift)).astype(BF16)
    for block, ref, pad in ((0, wqt, sz.pad_key), (2, wvt, sz.pad_head), (3, wgt, sz.pad_head)):
        part, shift, size = window(block)
        ref[...] = nt(pick((HEADS * pad, size), 0, pad, shift), part).astype(BF16)
    spec = (sz.rows, sz.width), 0, sz.pad_head, 0
    wo[...] = jnp.zeros(wo.shape, BF16)
    wo[:, : sz.width] = nn(pick(*spec), out[...]).astype(BF16)
    row = bias[...].reshape(1, sz.width)
    bias_col[...] = jnp.sum(jnp.where(hits(*spec), row, 0.0), axis=1, keepdims=True)


def attend(sz, groups, length, start_of, stride, per_group, gain, packed, work):
    wqt, wk, wvt, wgt, wo, bias_col = packed
    xs, ys, normed, queries, keys, values, gates, scores, weights, gated = work
    run = length // per_group
    factor = math.log2(math.e) / sz.head**0.5
    lane = lax.broadcasted_iota(jnp.int32, (1, sz.lanes), 1)
    inside = lane < sz.width
    gain_row = gain[...].reshape(1, sz.width)

    def places(group):
        return [pl.ds(start_of(group, c), run, stride=stride) for c in range(per_group)]

    def tokens_of(group):
        parts = [
            jnp.concatenate([xs[k, place, :] for place in places(group)], axis=0)
            for k in range(sz.chunks)
        ]
        return jnp.concatenate(parts, axis=1)

    for group in range(groups):
        x = tokens_of(group)
        mean = jnp.sum(x, axis=1, keepdims=True) * (1.0 / sz.width)
        centred = jnp.where(inside, x - mean, 0.0)
        spread = jnp.sum(centred * centred, axis=1, keepdims=True) * (1.0 / sz.width)
        value = centred[:, : sz.width] * lax.rsqrt(spread + 1e-05) * gain_row
        normed[group * length : (group + 1) * length] = value.astype(BF16)
    z = normed[...]
    feature = lax.broadcasted_iota(jnp.int32, (sz.rows, 1), 0)
    ones_row = jnp.where(feature % sz.pad_head == sz.head, 1.0, 0.0)
    queries[...] = (nt(wqt[...], z) * factor).astype(BF16)
    keys[...] = nn(z, wk[...]).astype(BF16)
    values[...] = (nt(wvt[...], z) + ones_row).astype(BF16)
    gates[...] = jax.nn.sigmoid(nt(wgt[...], z) + bias_col[...])
    pack = LANES // sz.pad_key
    zeros = jnp.zeros((sz.pad_key, length), BF16)

    def score(group):
        mine = slice(group * length, (group + 1) * length)
        for first in range(0, HEADS, pack):
            blocks = []
            for j in range(pack):
                low = (first + j) * sz.pad_key
                own = queries[low : low + sz.pad_key, mine]
                blocks.append(
                    jnp.concatenate([own if i == j else zeros for i in range(pack)], axis=1)
                )
            lanes = slice(first * sz.pad_key, (first + pack) * sz.pad_key)
            scores[group % 2, :, first * length : (first + pack) * length] = nn(
                keys[mine, lanes], jnp.concatenate(blocks, axis=0)
            )

    def soften(group):
        for head in range(HEADS):
            lanes = slice(head * length, (head + 1) * length)
            s = scores[group % 2, :, lanes]
            top = jnp.max(s, axis=0, keepdims=True)
            weights[group % 2, :, lanes] = jnp.exp2(s - top).astype(BF16)

    def mix(group):
        mine = slice(group * length, (group + 1) * length)
        for head in range(HEADS):
            rows = slice(head * sz.pad_head, (head + 1) * sz.pad_head)
            lanes = slice(head * length, (head + 1) * length)
            mixed = nn(values[rows, mine], weights[group % 2, :, lanes])
            total = mixed[sz.head : sz.head + 1]
            gated[rows, mine] = (mixed * (1.0 / total) * gates[rows, mine]).astype(BF16)

    score(0)
    for group in range(groups):
        if group + 1 < groups:
            score(group + 1)
        soften(group)
        mix(group)
    for group in range(groups):
        mine = slice(group * length, (group + 1) * length)
        y = tokens_of(group) + tn(gated[:, mine], wo[...])
        for k in range(sz.chunks):
            part = y[:, k * LANES : (k + 1) * LANES]
            for c, place in enumerate(places(group)):
                ys[k, place, :] = part[c * run : (c + 1) * run]


def spread_tokens(sz, source, xs):
    tokens = xs.shape[1]
    flat = source[...].astype(F32).reshape(tokens, sz.width)
    for k in range(sz.chunks):
        part = flat[:, k * LANES : min((k + 1) * LANES, sz.width)]
        if part.shape[1] < LANES:
            pad = jnp.zeros((tokens, LANES - part.shape[1]), F32)
            part = jnp.concatenate([part, pad], axis=1)
        xs[k] = part


def gather_tokens(sz, ys, target):
    shape = target.shape
    for k in range(sz.chunks):
        low, high = k * LANES, min((k + 1) * LANES, sz.width)
        part = ys[k][:, : high - low]
        target[..., low:high] = part.reshape(shape[:-1] + (high - low,)).astype(BF16)


def row_kernel(sz, n, rows, cols, *refs):
    x_ref, gain, *own_weights = refs[:5]
    next_weights = refs[5:8]
    result, *next_packed = refs[8:15]
    got, back, *rest = refs[15:]
    packed, rest = rest[:6], rest[6:]
    work = rest[:10]
    send_a, recv_a, send_b, recv_b, local_sem = rest[10:]
    me = lax.axis_index("row")
    block = rows * cols

    barrier = pltpu.get_barrier_semaphore()

    def greet(step, carry):
        peer = lax.rem(me + step, n)
        pl.semaphore_signal(barrier, inc=1, device_id={"row": peer}, device_id_type=MESH)
        return carry

    lax.fori_loop(1, n, greet, 0)
    pl.semaphore_wait(barrier, n - 1)

    def exchange(source, target, place, send, recv, body):
        def copy(peer, slot):
            return pltpu.make_async_remote_copy(
                src_ref=source.at[place(peer)],
                dst_ref=target.at[place(slot)],
                send_sem=send.at[peer],
                recv_sem=recv.at[slot],
                device_id={"row": peer},
                device_id_type=MESH,
            )

        def start(step, carry):
            copy(lax.rem(me + step, n), me).start()
            return carry

        lax.fori_loop(1, n, start, 0)
        own = pltpu.make_async_copy(source.at[place(me)], target.at[place(me)], local_sem)
        own.start()
        body()
        own.wait()

        def finish(step, carry):
            peer = lax.rem(me + step, n)
            copy(peer, me).wait_send()
            copy(peer, peer).wait_recv()
            return carry

        lax.fori_loop(1, n, finish, 0)

    exchange(
        x_ref,
        got,
        lambda device: pl.ds(device * rows, rows),
        send_a,
        recv_a,
        lambda: prepare(sz, own_weights, packed),
    )
    spread_tokens(sz, got, work[0])
    attend(
        sz, rows, n * cols, lambda g, c: g * cols + c, block, cols, gain, packed, work
    )
    gather_tokens(sz, work[1], back)
    exchange(
        back,
        result,
        lambda device: device,
        send_b,
        recv_b,
        lambda: prepare(sz, next_weights, next_packed),
    )


def col_kernel(sz, cols, x_ref, gain, *refs):
    packed, result, work = refs[:6], refs[6], refs[7:]
    spread_tokens(sz, x_ref, work[0])
    length = work[0].shape[1] // cols
    attend(sz, cols, length, lambda g, c: g, cols, 1, gain, packed, work)
    gather_tokens(sz, work[1], result)


VMEM = pl.BlockSpec(memory_space=pltpu.VMEM)


def per_device(
    pair_map, row_gain, row_proj, row_gate_bias, row_out, col_gain, col_proj, col_gate_bias, col_out
):
    local_rows, local_cols, width = pair_map.shape
    n = lax.axis_size("row")
    sz = Sizes(width)
    rows = local_rows // n
    tokens = local_rows * local_cols
    block = rows * local_cols
    shape = (n, block, width)
    done, *packed = pl.pallas_call(
        functools.partial(row_kernel, sz, n, rows, local_cols),
        out_shape=[jax.ShapeDtypeStruct(shape, BF16)]
        + [jax.ShapeDtypeStruct(*spec) for spec in sz.packed_shapes()],
        in_specs=[VMEM] * 8,
        out_specs=[VMEM] * 7,
        scratch_shapes=[pltpu.VMEM(pair_map.shape, BF16), pltpu.VMEM(shape, BF16)]
        + [pltpu.VMEM(*spec) for spec in sz.packed_shapes()]
        + sz.work_scratch(tokens, n * local_cols)
        + [pltpu.SemaphoreType.DMA((n,))] * 4
        + [pltpu.SemaphoreType.DMA],
        compiler_params=pltpu.CompilerParams(collective_id=0, has_side_effects=True),
        name="row_attention",
    )(pair_map, row_gain, row_proj, row_gate_bias, row_out, col_proj, col_gate_bias, col_out)
    splits = lax.axis_size("col")
    if splits > 1:
        done = done.reshape(local_rows, local_cols, width)
        done = lax.all_to_all(done, "col", split_axis=1, concat_axis=0, tiled=True)
        done = done.reshape(shape)
    cols = local_cols // splits
    full = tokens // cols
    updated = pl.pallas_call(
        functools.partial(col_kernel, sz, cols),
        out_shape=jax.ShapeDtypeStruct((full, cols, width), BF16),
        in_specs=[VMEM] * 8,
        out_specs=VMEM,
        scratch_shapes=sz.work_scratch(tokens, full),
        name="col_attention",
    )(done, col_gain, *packed)
    if splits > 1:
        updated = lax.all_to_all(updated, "col", split_axis=0, concat_axis=1, tiled=True)
    return updated


def solution(mesh):
    return jax.shard_map(
        per_device,
        mesh=mesh,
        in_specs=(P(("groups", "col"), "row", None), P(), P(), P(), P(), P(), P(), P(), P()),
        out_specs=P(("groups", "col"), "row", None),
        check_vma=False,
    )
```

time: 55.7 us -> 41.5 us (0.75)
  Pallas kernels: 48.6 us -> 37.5 us
  local copies, waits for them, and re-layouts: 6.75 us -> 3.82 us
    pallas_call x1, Pallas kernels: 11.5 us -> 5.02 us  [per_device(): pl.pallas_call(functools.partial(col_kernel, sz, cols), out_shape=jax.Sha...]
    reshape x7 -> x0, local copies, waits for them, and re-layouts: 5.3 us -> none  [the longest x2 2.09 us: per_device(): return updated.reshape(local_rows, local_cols, width)]
    pallas_call x1, Pallas kernels: 37.1 us -> 32.4 us  [per_device(): pl.pallas_call(functools.partial(row_kernel, sz, n, rows, local_cols), ou...]
    pallas_call x0 -> x1, local copies, waits for them, and re-layouts: none -> 1.92 us  [per_device(): pl.pallas_call(functools.partial(col_kernel, sz, cols), out_shape=jax.Sha...]
    unnamed x9 -> x1, local copies, waits for them, and re-layouts: 1.44 us -> 1.9 us
where the time goes in v2:
time: 41.5 us; the launch traced here: 41.3 us
  Pallas kernels  37.5 us (90%)
  local copies, waits for them, and re-layouts  3.82 us (9%)
    pallas_call x1, Pallas kernels, per_device(): pl.pallas_call(functools.partial(row_kernel, sz, n, rows, local_cols), ou...  32.4 us
    pallas_call x1, Pallas kernels, per_device(): pl.pallas_call(functools.partial(col_kernel, sz, cols), out_shape=jax.Sha...  5.02 us
    pallas_call x1, local copies, waits for them, and re-layouts, per_device(): pl.pallas_call(functools.partial(col_kernel, sz, cols), out_shape=jax.Sha...  1.92 us
    unnamed x1, local copies, waits for them, and re-layouts  1.9 us

profile of v2, /device:TPU:29, one launch (start us, length us, event | category | flops | bytes accessed | tf_op | source)
XLA Modules:
  0.0 41.3 jit_solution(7334214855903538997)
XLA Ops:
  0.0 1.9 %copy.10.refs_0_ = bf16[128,4,288]{2,1,0:T(4,128)(2,1)} copy(bf16[128,4,288]{0,2,1:T(8,128)(2,1)} %param.9) | data formatting | bytes 589824 | tf_op args[0]
  1.9 32.4 %row_attention.1 = (bf16[32,16,288]{2,1,0:T(8,128)(2,1)}, bf16[512,288]{1,0:T(8,128)(2,1)}, bf16[288,512]{1,0:T(8,128)(2,1)}, bf16[384,288]{1,0:T(8,128)(2,1)}, ...) custom-call(bf16[128,4,288]{2,1,0:T(4,128)(2,1)} %copy.10.refs_0_, f32[288]{0:T(512)} %refs_1_.1, ...), custom_call_target="tpu_custom_call" | custom-call | tf_op jit(solution)/shard_map/row_attention/pallas_call | solution.py:298
  34.4 5.0 %col_attention.1 = bf16[128,4,288]{2,1,0:T(4,128)(2,1)} custom-call(bf16[32,16,288]{2,1,0:T(8,128)(2,1)} %get-tuple-element.12.x_ref, f32[288]{0:T(512)} %gain.1, bf16[512,288]{1,0:T(8,128)(2,1)} %get-tuple-element.13.refs_0_, bf16[288,512]{1,0:T(8,128)(2,1)} %get-tuple-element.14.refs_1_, bf16[384,288]{1,0:T(8,128)(2,1)} %get-tuple-element.15.refs_2_, ...), custom_call_target="tpu_custom_call" | custom-call | tf_op jit(solution)/shard_map/col_attention/pallas_call | solution.py:319
  39.4 1.9 %copy.11 = bf16[128,4,288]{0,2,1:T(8,128)(2,1)} copy(bf16[128,4,288]{2,1,0:T(4,128)(2,1)} %col_attention.1) | data formatting | bytes 589824 | tf_op jit(solution)/shard_map/col_attention/pallas_call | solution.py:319

commit v3 on v2

--- a/solution.py
+++ b/solution.py
@@ -43,6 +43,13 @@
         self.keys = HEADS * self.pad_key
         self.lanes = ceil_to(width, LANES)
         self.chunks = self.lanes // LANES
+        self.full = width // LANES
+        self.rest = width % LANES
+        self.side = LANES // self.rest if self.rest else 1
+
+    def packed_rows(self, block):
+        assert self.rest == 0 or (LANES % self.rest == 0 and block % self.side == 0)
+        return self.full * block + (block // self.side if self.rest else 0)
 
     def packed_shapes(self):
         return [
@@ -100,7 +107,7 @@
     bias_col[...] = jnp.sum(jnp.where(hits(*spec), row, 0.0), axis=1, keepdims=True)
 
 
-def attend(sz, groups, length, start_of, stride, per_group, gain, packed, work):
+def attend(sz, groups, length, start_of, stride, per_group, gain, packed, work, emit=None):
     wqt, wk, wvt, wgt, wo, bias_col = packed
     xs, ys, normed, queries, keys, values, gates, scores, weights, gated = work
     run = length // per_group
@@ -176,36 +183,70 @@
     for group in range(groups):
         mine = slice(group * length, (group + 1) * length)
         y = tokens_of(group) + tn(gated[:, mine], wo[...])
+        if emit is not None:
+            emit(group, y)
+            continue
         for k in range(sz.chunks):
             part = y[:, k * LANES : (k + 1) * LANES]
             for c, place in enumerate(places(group)):
                 ys[k, place, :] = part[c * run : (c + 1) * run]
 
 
-def spread_tokens(sz, source, xs):
+def pack_tokens(sz, ys, target):
+    tokens = ys.shape[1]
+    n = target.shape[0]
+    block = tokens // n
+    for k in range(sz.full):
+        part = ys[k].reshape(n, block, LANES)
+        target[:, k * block : (k + 1) * block, :] = part.astype(BF16)
+    if sz.rest:
+        joined = None
+        for q in range(sz.side):
+            part = ys[sz.full, pl.ds(q, tokens // sz.side, stride=sz.side), :]
+            part = pltpu.roll(part, q * sz.rest, 1) if q else part
+            joined = part if joined is None else joined + part
+        part = joined.reshape(n, block // sz.side, LANES)
+        target[:, sz.full * block :, :] = part.astype(BF16)
+
+
+def unpack_tokens(sz, source, xs):
     tokens = xs.shape[1]
-    flat = source[...].astype(F32).reshape(tokens, sz.width)
+    n = source.shape[0]
+    block = tokens // n
+    for k in range(sz.full):
+        part = source[:, k * block : (k + 1) * block, :]
+        xs[k] = part.astype(F32).reshape(tokens, LANES)
+    if sz.rest:
+        joined = source[:, sz.full * block :, :].astype(F32).reshape(tokens // sz.side, LANES)
+        inside = lax.broadcasted_iota(jnp.int32, (1, LANES), 1) < sz.rest
+        for q in range(sz.side):
+            part = pltpu.roll(joined, LANES - q * sz.rest, 1) if q else joined
+            place = pl.ds(q, tokens // sz.side, stride=sz.side)
+            xs[sz.full, place, :] = jnp.where(inside, part, 0.0)
+
+
+def turn_tokens(sz, n, rows, source, xs, ys):
+    cols, width, length = source.shape
+    for c in range(cols):
+        turned = source[c].astype(F32).T
+        for k in range(sz.chunks):
+            part = turned[:, k * LANES : min((k + 1) * LANES, width)]
+            if part.shape[1] < LANES:
+                pad = jnp.zeros((length, LANES - part.shape[1]), F32)
+                part = jnp.concatenate([part, pad], axis=1)
+            xs[k, c * length : (c + 1) * length] = part
     for k in range(sz.chunks):
-        part = flat[:, k * LANES : min((k + 1) * LANES, sz.width)]
-        if part.shape[1] < LANES:
-            pad = jnp.zeros((tokens, LANES - part.shape[1]), F32)
-            part = jnp.concatenate([part, pad], axis=1)
-        xs[k] = part
-
-
-def gather_tokens(sz, ys, target):
-    shape = target.shape
-    for k in range(sz.chunks):
-        low, high = k * LANES, min((k + 1) * LANES, sz.width)
-        part = ys[k][:, : high - low]
-        target[..., low:high] = part.reshape(shape[:-1] + (high - low,)).astype(BF16)
+        for c in range(cols):
+            for r in range(rows):
+                part = xs[k, pl.ds(c * length + r, n, stride=rows), :]
+                ys[k, pl.ds(r * cols + c, n, stride=rows * cols), :] = part
 
 
 def row_kernel(sz, n, rows, cols, *refs):
     x_ref, gain, *own_weights = refs[:5]
     next_weights = refs[5:8]
     result, *next_packed = refs[8:15]
-    got, back, *rest = refs[15:]
+    sent, got, back, *rest = refs[15:]
     packed, rest = rest[:6], rest[6:]
     work = rest[:10]
     send_a, recv_a, send_b, recv_b, local_sem = rest[10:]
@@ -220,13 +261,15 @@
         return carry
 
     lax.fori_loop(1, n, greet, 0)
+    turn_tokens(sz, n, rows, x_ref, work[0], work[1])
+    pack_tokens(sz, work[1], sent)
     pl.semaphore_wait(barrier, n - 1)
 
-    def exchange(source, target, place, send, recv, body):
+    def exchange(source, target, send, recv, body):
         def copy(peer, slot):
             return pltpu.make_async_remote_copy(
-                src_ref=source.at[place(peer)],
-                dst_ref=target.at[place(slot)],
+                src_ref=source.at[peer],
+                dst_ref=target.at[slot],
                 send_sem=send.at[peer],
                 recv_sem=recv.at[slot],
                 device_id={"row": peer},
@@ -238,7 +281,7 @@
             return carry
 
         lax.fori_loop(1, n, start, 0)
-        own = pltpu.make_async_copy(source.at[place(me)], target.at[place(me)], local_sem)
+        own = pltpu.make_async_copy(source.at[me], target.at[me], local_sem)
         own.start()
         body()
         own.wait()
@@ -252,22 +295,20 @@
         lax.fori_loop(1, n, finish, 0)
 
     exchange(
-        x_ref,
+        sent,
         got,
-        lambda device: pl.ds(device * rows, rows),
         send_a,
         recv_a,
         lambda: prepare(sz, own_weights, packed),
     )
-    spread_tokens(sz, got, work[0])
+    unpack_tokens(sz, got, work[0])
     attend(
         sz, rows, n * cols, lambda g, c: g * cols + c, block, cols, gain, packed, work
     )
-    gather_tokens(sz, work[1], back)
+    pack_tokens(sz, work[1], back)
     exchange(
         back,
         result,
-        lambda device: device,
         send_b,
         recv_b,
         lambda: prepare(sz, next_weights, next_packed),
@@ -276,10 +317,27 @@
 
 def col_kernel(sz, cols, x_ref, gain, *refs):
     packed, result, work = refs[:6], refs[6], refs[7:]
-    spread_tokens(sz, x_ref, work[0])
+    unpack_tokens(sz, x_ref, work[0])
     length = work[0].shape[1] // cols
-    attend(sz, cols, length, lambda g, c: g, cols, 1, gain, packed, work)
-    gather_tokens(sz, work[1], result)
+
+    def emit(group, y):
+        result[group] = y[:, : sz.width].T.astype(BF16)
+
+    attend(sz, cols, length, lambda g, c: g, cols, 1, gain, packed, work, emit)
+
+
+def swap_columns(sz, done, block, rows, cols):
+    n = done.shape[0]
+    parts = [done[:, k * block : (k + 1) * block] for k in range(sz.full)]
+    if sz.rest:
+        parts.append(done[:, sz.full * block :].reshape(n, block, sz.rest))
+    whole = jnp.concatenate(parts, -1).reshape(rows, cols, sz.width)
+    whole = lax.all_to_all(whole, "col", split_axis=1, concat_axis=0, tiled=True)
+    whole = whole.reshape(n, block, sz.width)
+    parts = [whole[..., k * LANES : (k + 1) * LANES] for k in range(sz.full)]
+    if sz.rest:
+        parts.append(whole[..., sz.full * LANES :].reshape(n, block // sz.side, LANES))
+    return jnp.concatenate(parts, 1)
 
 
 VMEM = pl.BlockSpec(memory_space=pltpu.VMEM)
@@ -294,36 +352,36 @@
     rows = local_rows // n
     tokens = local_rows * local_cols
     block = rows * local_cols
-    shape = (n, block, width)
+    shape = (n, sz.packed_rows(block), LANES)
+    turned = jnp.transpose(pair_map, (1, 2, 0))
     done, *packed = pl.pallas_call(
         functools.partial(row_kernel, sz, n, rows, local_cols),
         out_shape=[jax.ShapeDtypeStruct(shape, BF16)]
         + [jax.ShapeDtypeStruct(*spec) for spec in sz.packed_shapes()],
         in_specs=[VMEM] * 8,
         out_specs=[VMEM] * 7,
-        scratch_shapes=[pltpu.VMEM(pair_map.shape, BF16), pltpu.VMEM(shape, BF16)]
+        scratch_shapes=[pltpu.VMEM(shape, BF16)] * 3
         + [pltpu.VMEM(*spec) for spec in sz.packed_shapes()]
         + sz.work_scratch(tokens, n * local_cols)
         + [pltpu.SemaphoreType.DMA((n,))] * 4
         + [pltpu.SemaphoreType.DMA],
         compiler_params=pltpu.CompilerParams(collective_id=0, has_side_effects=True),
         name="row_attention",
-    )(pair_map, row_gain, row_proj, row_gate_bias, row_out, col_proj, col_gate_bias, col_out)
+    )(turned, row_gain, row_proj, row_gate_bias, row_out, col_proj, col_gate_bias, col_out)
     splits = lax.axis_size("col")
     if splits > 1:
-        done = done.reshape(local_rows, local_cols, width)
-        done = lax.all_to_all(done, "col", split_axis=1, concat_axis=0, tiled=True)
-        done = done.reshape(shape)
+        done = swap_columns(sz, done, block, local_rows, local_cols)
     cols = local_cols // splits
     full = tokens // cols
     updated = pl.pallas_call(
         functools.partial(col_kernel, sz, cols),
-        out_shape=jax.ShapeDtypeStruct((full, cols, width), BF16),
+        out_shape=jax.ShapeDtypeStruct((cols, width, full), BF16),
         in_specs=[VMEM] * 8,
         out_specs=VMEM,
         scratch_shapes=sz.work_scratch(tokens, full),
         name="col_attention",
     )(done, col_gain, *packed)
+    updated = jnp.transpose(updated, (2, 0, 1))
     if splits > 1:
         updated = lax.all_to_all(updated, "col", split_axis=0, concat_axis=1, tiled=True)
     return updated

time: 41.5 us -> 35.2 us (0.85)
  the two profiles are of different devices: /device:TPU:29 before, /device:TPU:25 now
where the time goes in v3:
time: 35.2 us; the launch traced here: 35 us
  Pallas kernels  35 us (99%)
    pallas_call x1, Pallas kernels, per_device(): pl.pallas_call(functools.partial(row_kernel, sz, n, rows, local_cols), ou...  29.9 us
    pallas_call x1, Pallas kernels, per_device(): pl.pallas_call(functools.partial(col_kernel, sz, cols), out_shape=jax.Sha...  5.1 us

profile of v3, /device:TPU:25, one launch (start us, length us, event | category | flops | bytes accessed | tf_op | source)
XLA Modules:
  0.0 35.0 jit_solution(14635446029945603269)
XLA Ops:
  0.0 29.9 %row_attention.1 = (bf16[32,36,128]{2,1,0:T(8,128)(2,1)}, bf16[512,288]{1,0:T(8,128)(2,1)}, bf16[288,512]{1,0:T(8,128)(2,1)}, bf16[384,288]{1,0:T(8,128)(2,1)}, ...) custom-call(bf16[4,288,128]{2,1,0:T(8,128)(2,1)} %bitcast.2, f32[288]{0:T(512)} %refs_1_.1, ...), custom_call_target="tpu_custom_call" | custom-call | tf_op jit(solution)/shard_map/row_attention/pallas_call | solution.py:357
  29.9 5.1 %col_attention.1 = bf16[4,288,128]{2,1,0:T(8,128)(2,1)} custom-call(bf16[32,36,128]{2,1,0:T(8,128)(2,1)} %get-tuple-element.12.x_ref, f32[288]{0:T(512)} %gain.1, bf16[512,288]{1,0:T(8,128)(2,1)} %get-tuple-element.13.refs_0_, bf16[288,512]{1,0:T(8,128)(2,1)} %get-tuple-element.14.refs_1_, bf16[384,288]{1,0:T(8,128)(2,1)} %get-tuple-element.15.refs_2_, ...), custom_call_target="tpu_custom_call" | custom-call | tf_op jit(solution)/shard_map/col_attention/pallas_call | solution.py:376

commit v4 on v3

--- a/solution.py
+++ b/solution.py
@@ -107,7 +107,7 @@
     bias_col[...] = jnp.sum(jnp.where(hits(*spec), row, 0.0), axis=1, keepdims=True)
 
 
-def attend(sz, groups, length, start_of, stride, per_group, gain, packed, work, emit=None):
+def attend(sz, first, last, length, start_of, stride, per_group, gain, packed, work, emit=None):
     wqt, wk, wvt, wgt, wo, bias_col = packed
     xs, ys, normed, queries, keys, values, gates, scores, weights, gated = work
     run = length // per_group
@@ -126,35 +126,36 @@
         ]
         return jnp.concatenate(parts, axis=1)
 
-    for group in range(groups):
+    for group in range(first, last):
         x = tokens_of(group)
         mean = jnp.sum(x, axis=1, keepdims=True) * (1.0 / sz.width)
         centred = jnp.where(inside, x - mean, 0.0)
         spread = jnp.sum(centred * centred, axis=1, keepdims=True) * (1.0 / sz.width)
         value = centred[:, : sz.width] * lax.rsqrt(spread + 1e-05) * gain_row
         normed[group * length : (group + 1) * length] = value.astype(BF16)
-    z = normed[...]
+    here = slice(first * length, last * length)
+    z = normed[here]
     feature = lax.broadcasted_iota(jnp.int32, (sz.rows, 1), 0)
     ones_row = jnp.where(feature % sz.pad_head == sz.head, 1.0, 0.0)
-    queries[...] = (nt(wqt[...], z) * factor).astype(BF16)
-    keys[...] = nn(z, wk[...]).astype(BF16)
-    values[...] = (nt(wvt[...], z) + ones_row).astype(BF16)
-    gates[...] = jax.nn.sigmoid(nt(wgt[...], z) + bias_col[...])
+    queries[:, here] = (nt(wqt[...], z) * factor).astype(BF16)
+    keys[here] = nn(z, wk[...]).astype(BF16)
+    values[:, here] = (nt(wvt[...], z) + ones_row).astype(BF16)
+    gates[:, here] = jax.nn.sigmoid(nt(wgt[...], z) + bias_col[...])
     pack = LANES // sz.pad_key
     zeros = jnp.zeros((sz.pad_key, length), BF16)
 
     def score(group):
         mine = slice(group * length, (group + 1) * length)
-        for first in range(0, HEADS, pack):
+        for start in range(0, HEADS, pack):
             blocks = []
             for j in range(pack):
-                low = (first + j) * sz.pad_key
+                low = (start + j) * sz.pad_key
                 own = queries[low : low + sz.pad_key, mine]
                 blocks.append(
                     jnp.concatenate([own if i == j else zeros for i in range(pack)], axis=1)
                 )
-            lanes = slice(first * sz.pad_key, (first + pack) * sz.pad_key)
-            scores[group % 2, :, first * length : (first + pack) * length] = nn(
+            lanes = slice(start * sz.pad_key, (start + pack) * sz.pad_key)
+            scores[group % 2, :, start * length : (start + pack) * length] = nn(
                 keys[mine, lanes], jnp.concatenate(blocks, axis=0)
             )
 
@@ -174,13 +175,13 @@
             total = mixed[sz.head : sz.head + 1]
             gated[rows, mine] = (mixed * (1.0 / total) * gates[rows, mine]).astype(BF16)
 
-    score(0)
-    for group in range(groups):
-        if group + 1 < groups:
+    score(first)
+    for group in range(first, last):
+        if group + 1 < last:
             score(group + 1)
         soften(group)
         mix(group)
-    for group in range(groups):
+    for group in range(first, last):
         mine = slice(group * length, (group + 1) * length)
         y = tokens_of(group) + tn(gated[:, mine], wo[...])
         if emit is not None:
@@ -192,40 +193,38 @@
                 ys[k, place, :] = part[c * run : (c + 1) * run]
 
 
-def pack_tokens(sz, ys, target):
-    tokens = ys.shape[1]
+def pack_tokens(sz, ys, base, tokens, target):
     n = target.shape[0]
     block = tokens // n
     for k in range(sz.full):
-        part = ys[k].reshape(n, block, LANES)
+        part = ys[k, base : base + tokens].reshape(n, block, LANES)
         target[:, k * block : (k + 1) * block, :] = part.astype(BF16)
     if sz.rest:
         joined = None
         for q in range(sz.side):
-            part = ys[sz.full, pl.ds(q, tokens // sz.side, stride=sz.side), :]
+            part = ys[sz.full, pl.ds(base + q, tokens // sz.side, stride=sz.side), :]
             part = pltpu.roll(part, q * sz.rest, 1) if q else part
             joined = part if joined is None else joined + part
         part = joined.reshape(n, block // sz.side, LANES)
         target[:, sz.full * block :, :] = part.astype(BF16)
 
 
-def unpack_tokens(sz, source, xs):
-    tokens = xs.shape[1]
+def unpack_tokens(sz, source, xs, base, tokens):
     n = source.shape[0]
     block = tokens // n
     for k in range(sz.full):
         part = source[:, k * block : (k + 1) * block, :]
-        xs[k] = part.astype(F32).reshape(tokens, LANES)
+        xs[k, base : base + tokens] = part.astype(F32).reshape(tokens, LANES)
     if sz.rest:
         joined = source[:, sz.full * block :, :].astype(F32).reshape(tokens // sz.side, LANES)
         inside = lax.broadcasted_iota(jnp.int32, (1, LANES), 1) < sz.rest
         for q in range(sz.side):
             part = pltpu.roll(joined, LANES - q * sz.rest, 1) if q else joined
-            place = pl.ds(q, tokens // sz.side, stride=sz.side)
+            place = pl.ds(base + q, tokens // sz.side, stride=sz.side)
             xs[sz.full, place, :] = jnp.where(inside, part, 0.0)
 
 
-def turn_tokens(sz, n, rows, source, xs, ys):
+def turn_tokens(sz, n, rows, span, source, xs, ys):
     cols, width, length = source.shape
     for c in range(cols):
         turned = source[c].astype(F32).T
@@ -239,7 +238,12 @@
         for c in range(cols):
             for r in range(rows):
                 part = xs[k, pl.ds(c * length + r, n, stride=rows), :]
-                ys[k, pl.ds(r * cols + c, n, stride=rows * cols), :] = part
+                first = r // span * n * span * cols + r % span * cols + c
+                ys[k, pl.ds(first, n, stride=span * cols), :] = part
+
+
+def row_chunks(rows, cols):
+    return 2 if rows % 2 == 0 and rows // 2 * cols % 8 == 0 else 1
 
 
 def row_kernel(sz, n, rows, cols, *refs):
@@ -249,9 +253,11 @@
     sent, got, back, *rest = refs[15:]
     packed, rest = rest[:6], rest[6:]
     work = rest[:10]
-    send_a, recv_a, send_b, recv_b, local_sem = rest[10:]
+    send_a, recv_a, send_b, recv_b, local_a, local_b = rest[10:]
     me = lax.axis_index("row")
-    block = rows * cols
+    chunks = row_chunks(rows, cols)
+    span = rows // chunks
+    tokens = n * span * cols
 
     barrier = pltpu.get_barrier_semaphore()
 
@@ -261,11 +267,12 @@
         return carry
 
     lax.fori_loop(1, n, greet, 0)
-    turn_tokens(sz, n, rows, x_ref, work[0], work[1])
-    pack_tokens(sz, work[1], sent)
+    turn_tokens(sz, n, rows, span, x_ref, work[0], work[1])
+    for h in range(chunks):
+        pack_tokens(sz, work[1], h * tokens, tokens, sent.at[h])
     pl.semaphore_wait(barrier, n - 1)
 
-    def exchange(source, target, send, recv, body):
+    def exchange(source, target, send, recv, local):
         def copy(peer, slot):
             return pltpu.make_async_remote_copy(
                 src_ref=source.at[peer],
@@ -276,68 +283,115 @@
                 device_id_type=MESH,
             )
 
-        def start(step, carry):
-            copy(lax.rem(me + step, n), me).start()
-            return carry
-
-        lax.fori_loop(1, n, start, 0)
-        own = pltpu.make_async_copy(source.at[me], target.at[me], local_sem)
-        own.start()
-        body()
-        own.wait()
-
-        def finish(step, carry):
-            peer = lax.rem(me + step, n)
-            copy(peer, me).wait_send()
-            copy(peer, peer).wait_recv()
-            return carry
-
-        lax.fori_loop(1, n, finish, 0)
-
-    exchange(
-        sent,
-        got,
-        send_a,
-        recv_a,
-        lambda: prepare(sz, own_weights, packed),
-    )
-    unpack_tokens(sz, got, work[0])
-    attend(
-        sz, rows, n * cols, lambda g, c: g * cols + c, block, cols, gain, packed, work
-    )
-    pack_tokens(sz, work[1], back)
-    exchange(
-        back,
-        result,
-        send_b,
-        recv_b,
-        lambda: prepare(sz, next_weights, next_packed),
-    )
-
-
-def col_kernel(sz, cols, x_ref, gain, *refs):
+        own = pltpu.make_async_copy(source.at[me], target.at[me], local)
+
+        def start():
+            def step_on(step, carry):
+                copy(lax.rem(me + step, n), me).start()
+                return carry
+
+            lax.fori_loop(1, n, step_on, 0)
+            own.start()
+
+        def arrive():
+            def step_on(step, carry):
+                peer = lax.rem(me + n - step, n)
+                copy(peer, peer).wait_recv()
+                return carry
+
+            own.wait()
+            lax.fori_loop(1, n, step_on, 0)
+
+        def leave():
+            def step_on(step, carry):
+                copy(lax.rem(me + step, n), me).wait_send()
+                return carry
+
+            lax.fori_loop(1, n, step_on, 0)
+
+        return start, arrive, leave
+
+    there = [
+        exchange(sent.at[h], got.at[h], send_a.at[h], recv_a.at[h], local_a.at[h])
+        for h in range(chunks)
+    ]
+    home = [
+        exchange(back.at[h], result.at[h], send_b.at[h], recv_b.at[h], local_b.at[h])
+        for h in range(chunks)
+    ]
+    for start, _, _ in there:
+        start()
+    prepare(sz, own_weights, packed)
+    for h in range(chunks):
+        there[h][1]()
+        unpack_tokens(sz, got.at[h], work[0], h * tokens, tokens)
+
+        def start_of(group, c):
+            return h * tokens + (group - h * span) * cols + c
+
+        attend(
+            sz,
+            h * span,
+            (h + 1) * span,
+            n * cols,
+            start_of,
+            span * cols,
+            cols,
+            gain,
+            packed,
+            work,
+        )
+        pack_tokens(sz, work[1], h * tokens, tokens, back.at[h])
+        home[h][0]()
+    prepare(sz, next_weights, next_packed)
+    for _, _, leave in there:
+        leave()
+    for _, arrive, leave in home:
+        arrive()
+        leave()
+
+
+def col_kernel(sz, cols, rows, row_cols, x_ref, gain, *refs):
     packed, result, work = refs[:6], refs[6], refs[7:]
-    unpack_tokens(sz, x_ref, work[0])
-    length = work[0].shape[1] // cols
+    xs, ys = work[:2]
+    chunks, n = x_ref.shape[:2]
+    tokens = xs.shape[1] // chunks
+    span = rows // chunks
+    landing = xs if chunks == 1 else ys
+    for h in range(chunks):
+        unpack_tokens(sz, x_ref.at[h], landing, h * tokens, tokens)
+        if chunks == 1:
+            continue
+        for k in range(sz.chunks):
+            for r in range(span):
+                for c in range(row_cols):
+                    part = ys[k, pl.ds(h * tokens + r * row_cols + c, n, stride=span * row_cols), :]
+                    first = (h * span + r) * row_cols + c
+                    xs[k, pl.ds(first, n, stride=rows * row_cols), :] = part
+    length = xs.shape[1] // cols
 
     def emit(group, y):
         result[group] = y[:, : sz.width].T.astype(BF16)
 
-    attend(sz, cols, length, lambda g, c: g, cols, 1, gain, packed, work, emit)
-
-
-def swap_columns(sz, done, block, rows, cols):
-    n = done.shape[0]
+    attend(sz, 0, cols, length, lambda g, c: g, cols, 1, gain, packed, work, emit)
+
+
+def swap_columns(sz, done, rows, cols):
+    chunks, n = done.shape[:2]
+    span = rows // n // chunks
+    block = span * cols
+    done = jnp.swapaxes(done, 0, 1).reshape((chunks * n,) + done.shape[2:])
     parts = [done[:, k * block : (k + 1) * block] for k in range(sz.full)]
     if sz.rest:
-        parts.append(done[:, sz.full * block :].reshape(n, block, sz.rest))
+        parts.append(done[:, sz.full * block :].reshape(chunks * n, block, sz.rest))
     whole = jnp.concatenate(parts, -1).reshape(rows, cols, sz.width)
     whole = lax.all_to_all(whole, "col", split_axis=1, concat_axis=0, tiled=True)
-    whole = whole.reshape(n, block, sz.width)
+    block = rows * cols // n
+    whole = whole.reshape(1, n, block, sz.width)
     parts = [whole[..., k * LANES : (k + 1) * LANES] for k in range(sz.full)]
     if sz.rest:
-        parts.append(whole[..., sz.full * LANES :].reshape(n, block // sz.side, LANES))
-    return jnp.concatenate(parts, 1)
+        parts.append(whole[..., sz.full * LANES :].reshape(1, n, block // sz.side, LANES))
+    return jnp.concatenate(parts, 2)
 
 
 VMEM = pl.BlockSpec(memory_space=pltpu.VMEM)
@@ -351,8 +405,8 @@
     sz = Sizes(width)
     rows = local_rows // n
     tokens = local_rows * local_cols
-    block = rows * local_cols
-    shape = (n, sz.packed_rows(block), LANES)
+    chunks = row_chunks(rows, local_cols)
+    shape = (chunks, n, sz.packed_rows(rows // chunks * local_cols), LANES)
     turned = jnp.transpose(pair_map, (1, 2, 0))
     done, *packed = pl.pallas_call(
         functools.partial(row_kernel, sz, n, rows, local_cols),
@@ -363,18 +417,18 @@
         scratch_shapes=[pltpu.VMEM(shape, BF16)] * 3
         + [pltpu.VMEM(*spec) for spec in sz.packed_shapes()]
         + sz.work_scratch(tokens, n * local_cols)
-        + [pltpu.SemaphoreType.DMA((n,))] * 4
-        + [pltpu.SemaphoreType.DMA],
+        + [pltpu.SemaphoreType.DMA((chunks, n))] * 4
+        + [pltpu.SemaphoreType.DMA((chunks,))] * 2,
         compiler_params=pltpu.CompilerParams(collective_id=0, has_side_effects=True),
         name="row_attention",
     )(turned, row_gain, row_proj, row_gate_bias, row_out, col_proj, col_gate_bias, col_out)
     splits = lax.axis_size("col")
     if splits > 1:
-        done = swap_columns(sz, done, block, local_rows, local_cols)
+        done = swap_columns(sz, done, local_rows, local_cols)
     cols = local_cols // splits
     full = tokens // cols
     updated = pl.pallas_call(
-        functools.partial(col_kernel, sz, cols),
+        functools.partial(col_kernel, sz, cols, rows, local_cols),
         out_shape=jax.ShapeDtypeStruct((cols, width, full), BF16),
         in_specs=[VMEM] * 8,
         out_specs=VMEM,

time: 35.2 us -> 37.9 us (1.077)
  the two profiles are of different devices: /device:TPU:25 before, /device:TPU:0 now
where the time goes in v4:
time: 37.9 us; the launch traced here: 37.7 us
  Pallas kernels  37.7 us (99%)
    pallas_call x1, Pallas kernels, per_device(): pl.pallas_call(functools.partial(row_kernel, sz, n, rows, local_cols), ou...  32.5 us
    pallas_call x1, Pallas kernels, per_device(): pl.pallas_call(functools.partial(col_kernel, sz, cols, rows, local_cols),...  5.25 us

profile of v4, /device:TPU:0, one launch (start us, length us, event | category | flops | bytes accessed | tf_op | source)
XLA Modules:
  0.0 37.7 jit_solution(18289957087901335461)
XLA Ops:
  0.0 32.5 %row_attention.1 = (bf16[2,32,18,128]{3,2,1,0:T(8,128)(2,1)}, bf16[512,288]{1,0:T(8,128)(2,1)}, bf16[288,512]{1,0:T(8,128)(2,1)}, bf16[384,288]{1,0:T(8,128)(2,1...) custom-call(bf16[4,288,128]{2,1,0:T(8,128)(2,1)} %bitcast.2, f32[288]{0:T(512)} %refs_1_.1, ...), custom_call_target="tpu_custom_call" | custom-call | tf_op jit(solution)/shard_map/row_attention/pallas_call | solution.py:411
  32.5 5.2 %col_attention.1 = bf16[4,288,128]{2,1,0:T(8,128)(2,1)} custom-call(bf16[2,32,18,128]{3,2,1,0:T(8,128)(2,1)} %get-tuple-element.12.x_ref, f32[288]{0:T(512)} %gain.1, bf16[512,288]{1,0:T(8,128)(2,1)} %get-tuple-element.13.refs_0_, bf16[288,512]{1,0:T(8,128)(2,1)} %get-tuple-element.14.refs_1_, bf16[384,288]{1,0:T(8,128)(2,1)} %get-tuple-element.15.refs_2_, ...), custom_call_target="tpu_custom_call" | custom-call | tf_op jit(solution)/shard_map/col_attention/pallas_call | solution.py:430

commit v5 on v3

--- a/solution.py
+++ b/solution.py
@@ -242,6 +242,21 @@
                 ys[k, pl.ds(r * cols + c, n, stride=rows * cols), :] = part
 
 
+def partners(me, n):
+    if n & (n - 1):
+        return [lax.rem(me + step, n) for step in range(1, n)]
+    shifts = []
+    weight = 1
+    while weight < n:
+        shifts.append(weight - 2 * weight * (me // weight % 2))
+        weight *= 2
+    flipped = {0: me}
+    for step in range(1, n):
+        high = step.bit_length() - 1
+        flipped[step] = flipped[step - (1 << high)] + shifts[high]
+    return [flipped[step] for step in range(n - 1, 0, -1)]
+
+
 def row_kernel(sz, n, rows, cols, *refs):
     x_ref, gain, *own_weights = refs[:5]
     next_weights = refs[5:8]
@@ -265,6 +280,8 @@
     pack_tokens(sz, work[1], sent)
     pl.semaphore_wait(barrier, n - 1)
 
+    peers = partners(me, n)
+
     def exchange(source, target, send, recv, body):
         def copy(peer, slot):
             return pltpu.make_async_remote_copy(
@@ -276,11 +293,8 @@
                 device_id_type=MESH,
             )
 
-        def start(step, carry):
-            copy(lax.rem(me + step, n), me).start()
-            return carry
-
-        lax.fori_loop(1, n, start, 0)
+        for peer in peers:
+            copy(peer, me).start()
         own = pltpu.make_async_copy(source.at[me], target.at[me], local_sem)
         own.start()
         body()

time: 35.2 us -> 36.1 us (1.026)
  the two profiles are of different devices: /device:TPU:25 before, /device:TPU:0 now
where the time goes in v5:
time: 36.1 us; the launch traced here: 36 us
  Pallas kernels  36 us (100%)
    pallas_call x1, Pallas kernels, per_device(): pl.pallas_call(functools.partial(row_kernel, sz, n, rows, local_cols), ou...  30.9 us
    pallas_call x1, Pallas kernels, per_device(): pl.pallas_call(functools.partial(col_kernel, sz, cols), out_shape=jax.Sha...  5.1 us

profile of v5, /device:TPU:0, one launch (start us, length us, event | category | flops | bytes accessed | tf_op | source)
XLA Modules:
  0.0 36.0 jit_solution(10477495590919366803)
XLA Ops:
  0.0 30.9 %row_attention.1 = (bf16[32,36,128]{2,1,0:T(8,128)(2,1)}, bf16[512,288]{1,0:T(8,128)(2,1)}, bf16[288,512]{1,0:T(8,128)(2,1)}, bf16[384,288]{1,0:T(8,128)(2,1)}, ...) custom-call(bf16[4,288,128]{2,1,0:T(8,128)(2,1)} %bitcast.2, f32[288]{0:T(512)} %refs_1_.1, ...), custom_call_target="tpu_custom_call" | custom-call | tf_op jit(solution)/shard_map/row_attention/pallas_call | solution.py:371
  30.9 5.1 %col_attention.1 = bf16[4,288,128]{2,1,0:T(8,128)(2,1)} custom-call(bf16[32,36,128]{2,1,0:T(8,128)(2,1)} %get-tuple-element.12.x_ref, f32[288]{0:T(512)} %gain.1, bf16[512,288]{1,0:T(8,128)(2,1)} %get-tuple-element.13.refs_0_, bf16[288,512]{1,0:T(8,128)(2,1)} %get-tuple-element.14.refs_1_, bf16[384,288]{1,0:T(8,128)(2,1)} %get-tuple-element.15.refs_2_, ...), custom_call_target="tpu_custom_call" | custom-call | tf_op jit(solution)/shard_map/col_attention/pallas_call | solution.py:390
